TPU v7x, 32 devices: a whole 2x2x4 slice. The times are simulated.
32 devices in a mesh: gx: 4 (over z), gy: 8 (over y, x, core).
Axes of the slice: x: 2, y: 2, z: 4, core: 2. Of those that a mesh axis runs over, the one named last changes fastest.
Arguments:
- flow: float32 [19, 32, 64, 512], P(None, 'gx', 'gy'), may hold values from 0.0116 to 0.467, as said below
- field: float32 [7, 32, 64, 512], P(None, 'gx', 'gy'), may hold values from -0.45 to 0.45, as said below
- adj_flow_in: float32 [19, 32, 64, 512], P(None, 'gx', 'gy'), may hold values from -6 to 6
- adj_field_in: float32 [7, 32, 64, 512], P(None, 'gx', 'gy'), may hold values from -6 to 6
- profile: float32 [32, 64, 512], P('gx', 'gy'), may hold values from 0.5 to 1.5
- strengths: float32 [32], replicated, may hold values from 0.5 to 2
- wall: int32 [32, 64, 512], P('gx', 'gy'), may hold values 0 or 1
- magnet: int32 [32, 64, 512], P('gx', 'gy'), may hold values from 0 to 31
Outputs:
- new_flow: float32 [19, 32, 64, 512], P(None, 'gx', 'gy')
- new_field: float32 [7, 32, 64, 512], P(None, 'gx', 'gy')
- adj_flow: float32 [19, 32, 64, 512], P(None, 'gx', 'gy')
- adj_field: float32 [7, 32, 64, 512], P(None, 'gx', 'gy')
- magnet_grad: float32 [32], replicated
Inputs may be any that keep to these rules, and one draw needn't show every extreme that they name: flow populations are positive, near w_i times a density of order one. field populations are v_k times a local field value plus noise.
All inputs are finite; a program needn't handle non-finite values. No bound on the sum of `wall` on one device may be relied on, other than what follows from the above.
Results may differ from a plain program's by a relative error of at most 0.00023.
Values sent between devices are 32-bit elements; how exact they have to be, the bound alone decides.
No kernel may reach another device: no remote copies, remote signals or barrier semaphores. Data moves between devices by JAX's collectives and lax.ppermute only.
A program may use at most 64 MiB of HBM per device.

v0:
```python
import math
import jax
import jax.numpy as jnp
import numpy as np
from jax import lax
from jax.sharding import PartitionSpec as P

LATTICE = np.array(
    [
        [0, 0, 0],
        [1, 0, 0],
        [-1, 0, 0],
        [0, 1, 0],
        [0, -1, 0],
        [0, 0, 1],
        [0, 0, -1],
        [1, 1, 0],
        [-1, -1, 0],
        [1, -1, 0],
        [-1, 1, 0],
        [1, 0, 1],
        [-1, 0, -1],
        [1, 0, -1],
        [-1, 0, 1],
        [0, 1, 1],
        [0, -1, -1],
        [0, 1, -1],
        [0, -1, 1],
    ]
)
OPPOSITE = [0, 2, 1, 4, 3, 6, 5, 8, 7, 10, 9, 12, 11, 14, 13, 16, 15, 18, 17]
WEIGHTS_FLOW = [1.0 / 3.0] + [1.0 / 18.0] * 6 + [1.0 / 36.0] * 12
WEIGHTS_FIELD = [0.25] + [0.125] * 6
OMEGA_PLUS = 1.25
OMEGA_MINUS = 1.0 / 1.125
TAU_PLUS = 0.8
COUPLE = 2.0
SOURCE = 2.0


def with_halo(block, sides, width):
    for axis, dim in sides:
        count = lax.axis_size(axis)
        forward = [(i, i + 1) for i in range(count - 1)]
        forward.append((count - 1, 0))
        backward = [(target, source) for source, target in forward]
        low = lax.ppermute(
            lax.slice_in_dim(block, block.shape[dim] - width, None, axis=dim), axis, forward
        )
        high = lax.ppermute(lax.slice_in_dim(block, 0, width, axis=dim), axis, backward)
        block = jnp.concatenate([low, block, high], axis=dim)
    return block


def column(values, ndim):
    return jnp.array([float(v) for v in values], jnp.float32).reshape(
        (len(values),) + (1,) * (ndim - 1)
    )


def collide(flow, field, bfield, fluid):
    ndim = flow.ndim
    velx = column(LATTICE[:, 0], ndim)
    vely = column(LATTICE[:, 1], ndim)
    velz = column(LATTICE[:, 2], ndim)
    weight = column(WEIGHTS_FLOW, ndim)
    weight_b = column(WEIGHTS_FIELD, ndim)
    rho = jnp.sum(flow, 0) + (1.0 - fluid)
    momx = jnp.sum(velx * flow, 0)
    momy = jnp.sum(vely * flow, 0)
    momz = jnp.sum(velz * flow, 0)
    speed_x = momx / rho
    speed_y = momy / rho
    speed_z = momz / rho
    bvalue = jnp.sum(field, 0)
    current = jnp.sum(vely[:7] * field, 0) - bvalue * speed_y
    shear = jnp.sum(velx * vely * flow, 0) - momx * speed_y
    force = COUPLE * bfield * current
    shifted = speed_x + TAU_PLUS * force / rho
    along = velx * shifted + vely * speed_y + velz * speed_z
    square = shifted * shifted + speed_y * speed_y + speed_z * speed_z
    equil = weight * rho * (1.0 + 3.0 * along + 4.5 * along * along - 1.5 * square)
    offset = flow - equil
    flipped = jnp.stack([offset[k] for k in OPPOSITE], 0)
    post_flow = (
        flow - 0.5 * OMEGA_PLUS * (offset + flipped) - 0.5 * OMEGA_MINUS * (offset - flipped)
    )
    along_b = velx[:7] * speed_x + vely[:7] * speed_y + velz[:7] * speed_z
    post_field = weight_b * bvalue * (1.0 + 4.0 * along_b) + weight_b * SOURCE * bfield * shear
    return (post_flow, post_field)


def pull_stream(pad_pops, pad_fluid, post, fluid, count):
    size_x, size_y, size_z = fluid.shape
    parts = []
    for i in range(count):
        cx, cy, cz = (int(v) for v in LATTICE[i])
        near = pad_fluid[
            1 - cx : 1 - cx + size_x, 1 - cy : 1 - cy + size_y, 1 - cz : 1 - cz + size_z
        ]
        moved = pad_pops[
            i, 1 - cx : 1 - cx + size_x, 1 - cy : 1 - cy + size_y, 1 - cz : 1 - cz + size_z
        ]
        parts.append(fluid * (near * moved + (1.0 - near) * post[OPPOSITE[i]]))
    return jnp.stack(parts, 0)


def push_adjoint(pad_pops, pad_fluid, local, fluid, count):
    size_x, size_y, size_z = fluid.shape
    parts = []
    for i in range(count):
        cx, cy, cz = (int(v) for v in LATTICE[i])
        near = pad_fluid[
            1 + cx : 1 + cx + size_x, 1 + cy : 1 + cy + size_y, 1 + cz : 1 + cz + size_z
        ]
        moved = pad_pops[
            i, 1 + cx : 1 + cx + size_x, 1 + cy : 1 + cy + size_y, 1 + cz : 1 + cz + size_z
        ]
        parts.append(fluid * (near * moved + (1.0 - near) * local[OPPOSITE[i]]))
    return jnp.stack(parts, 0)


def close_ends(padded):
    return jnp.pad(padded, ((0, 0), (0, 0), (0, 0), (1, 1)))


def wall_rims(pad_fluid):
    rows = lax.broadcasted_iota(jnp.int32, pad_fluid.shape, 1)
    here = lax.axis_index("gy")
    last = lax.axis_size("gy") - 1
    outside = (rows == 0) & (here == 0) | (rows == pad_fluid.shape[1] - 1) & (here == last)
    return jnp.where(outside, 0.0, pad_fluid)


def on_device(flow, field, adj_flow_in, adj_field_in, profile, strengths, wall, magnet):
    count_mag = strengths.shape[0]
    fluid = (1 - wall).astype(jnp.float32)
    table = (
        magnet[None] == lax.broadcasted_iota(jnp.int32, (count_mag,) + magnet.shape, 0)
    ).astype(jnp.float32)
    bcell = jnp.tensordot(strengths, table, axes=1, precision=lax.Precision.HIGHEST) * profile
    post_flow, post_field = collide(flow, field, bcell, fluid)
    joined = jnp.concatenate([post_flow, post_field, fluid[None]], 0)
    padded = close_ends(with_halo(joined, (("gx", 1), ("gy", 2)), 1))
    pad_fluid = wall_rims(padded[26])
    pad_state = padded[:26]
    incoming = jnp.concatenate([adj_flow_in, adj_field_in], 0)
    pad_adj = close_ends(with_halo(incoming, (("gx", 1), ("gy", 2)), 1))
    new_flow = pull_stream(pad_state[:19], pad_fluid, post_flow, fluid, 19)
    new_field = pull_stream(pad_state[19:], pad_fluid, post_field, fluid, 7)
    ast_flow = push_adjoint(pad_adj[:19], pad_fluid, adj_flow_in, fluid, 19)
    ast_field = push_adjoint(pad_adj[19:], pad_fluid, adj_field_in, fluid, 7)

    def local_collide(first, second, third):
        return collide(first, second, third, fluid)

    _, pullback = jax.vjp(local_collide, new_flow, new_field, bcell)
    adj_flow, adj_field, dcell = pullback((ast_flow, ast_field))
    shares = jnp.tensordot(table, dcell * profile, axes=3, precision=lax.Precision.HIGHEST)
    totals = lax.psum(shares, ("gx", "gy"))
    cells = (
        flow.shape[1] * lax.axis_size("gx") * flow.shape[2] * lax.axis_size("gy") * flow.shape[3]
    )
    magnet_grad = totals / math.sqrt(cells / count_mag)
    return (new_flow, new_field, adj_flow, adj_field, magnet_grad)


def solution(mesh):
    return jax.shard_map(
        on_device,
        mesh=mesh,
        in_specs=(
            P(None, "gx", "gy", None),
            P(None, "gx", "gy", None),
            P(None, "gx", "gy", None),
            P(None, "gx", "gy", None),
            P("gx", "gy", None),
            P(),
            P("gx", "gy", None),
            P("gx", "gy", None),
        ),
        out_specs=(
            P(None, "gx", "gy", None),
            P(None, "gx", "gy", None),
            P(None, "gx", "gy", None),
            P(None, "gx", "gy", None),
            P(),
        ),
        check_vma=False,
    )
```

profile of v0, /device:TPU:0, one launch (start us, length us, event | category | flops | bytes accessed | tf_op | source)
XLA Modules:
  0.0 164.3 jit_solution(2467456283072510997)
XLA Ops:
  0.7 2.0 %constant_dynamic-update-slice_fusion.46 = f32[26,8,8,512]{3,2,1,0:T(8,128)S(1)} fusion(f32[19,8,8,512]{3,2,1,0:T(8,128)} %param.20), kind=kLoop, calls=%fused_computation.129 | loop fusion | bytes 4980736
  2.8 1.0 fusion.254
  3.8 3.0 %collective-permute-start.5 = (f32[26,1,8,512]{3,2,1,0:T(8,128)}, f32[26,1,8,512]{3,2,1,0:T(8,128)}, u32[]{:S(2)}, u32[]{:S(2)}) collective-permute-start(f32[26,1,8,512]{3,2,1,0:T(8,128)} %get-tuple-element.112), channel_id=1, source_target_pairs={{0,8},{8,16},{16,24},{24,0},{1,9},{9,17},{17,25},{25,1},{2,10},{10... | collective-permute-start | bytes 1277960 | tf_op jit(solution)/shard_map/ppermute | solution.py:47
  6.8 2.1 %collective-permute-start.4 = (f32[26,1,8,512]{3,2,1,0:T(8,128)}, f32[26,1,8,512]{3,2,1,0:T(8,128)}, u32[]{:S(2)}, u32[]{:S(2)}) collective-permute-start(f32[26,1,8,512]{3,2,1,0:T(8,128)} %get-tuple-element.113), channel_id=1, source_target_pairs={{8,0},{16,8},{24,16},{0,24},{9,1},{17,9},{25,17},{1,25},{10,2},{18... | collective-permute-start | bytes 1277960 | tf_op jit(solution)/shard_map/ppermute | solution.py:50
  8.9 0.6 iota_compare_fusion.4
  9.6 0.1 fusion.238
  9.7 1.6 fusion.4
  11.4 1.0 multiply_reduce_fusion.7
  12.6 1.3 fusion.16
  14.3 1.8 %multiply_subtract_fusion = f32[19,8,8,512]{3,2,1,0:T(8,128)S(1)} fusion(f32[19,8,8,512]{3,2,1,0:T(8,128)S(1)} %constant_dynamic-update-slice_fusion, f32[19,8,8,512]{3,2,1,0:T(8,128)S(1)} %copy-done.7, f32[8,8,512]{2,1,0:T(8,128)S(1)} %get-tuple-element.77, f32[8,8,512]{2,1,0:T(8,128)S(1)} %get-tuple-element.81, f32[19]{0:T(128)S(1)} %copy-done.44, ...), kind=kLoop, calls=%fused_computation.48 | loop fusion | flops 12451840 | bytes 8126768 | tf_op jit(solution)/shard_map/sub | solution.py:86
  16.2 0.4 fusion.21
  16.7 0.6 copy-done.8
  17.3 1.0 pad_maximum_fusion.10
  18.3 3.8 %collective-permute-start.1 = (f32[27,1,8,512]{3,2,1,0:T(8,128)}, f32[27,1,8,512]{3,2,1,0:T(8,128)}, u32[]{:S(2)}, u32[]{:S(2)}) collective-permute-start(f32[27,1,8,512]{3,2,1,0:T(8,128)} %get-tuple-element.111), channel_id=1, source_target_pairs={{8,0},{16,8},{24,16},{0,24},{9,1},{17,9},{25,17},{1,25},{10,2},{18... | collective-permute-start | bytes 1327112 | tf_op jit(solution)/shard_map/ppermute | solution.py:50
  22.1 7.0 %collective-permute-done.4 = f32[26,1,8,512]{3,2,1,0:T(8,128)} collective-permute-done((f32[26,1,8,512]{3,2,1,0:T(8,128)}, f32[26,1,8,512]{3,2,1,0:T(8,128)}, u32[]{:S(2)}, u32[]{:S(2)}) %collective-permute-start.4) | collective-permute-done | bytes 426016 | tf_op jit(solution)/shard_map/ppermute | solution.py:50
  29.1 4.5 %pad_maximum_fusion.5 = (f32[26,10,1,512]{3,2,1,0:T(1,128)S(1)}, f32[26,10,1,512]{3,2,1,0:T(1,128)S(1)}) fusion(f32[26,1,8,512]{3,2,1,0:T(8,128)} %collective-permute-done.4, f32[26,8,8,512]{3,2,1,0:T(8,128)} %copy-done.2, f32[26,1,8,512]{3,2,1,0:T(8,128)} %collective-permute-done.5), kind=kLoop, calls=%fused_computation.72 | loop fusion | flops 532480 | bytes 5324800 | tf_op jit(solution)/shard_map/concatenate | solution.py:51
  33.7 2.6 %collective-permute-start.6 = (f32[26,10,1,512]{3,2,1,0:T(1,128)S(1)}, f32[26,10,1,512]{3,2,1,0:T(1,128)S(1)}, u32[]{:S(2)}, u32[]{:S(2)}) collective-permute-start(f32[26,10,1,512]{3,2,1,0:T(1,128)S(1)} %get-tuple-element.109), channel_id=1, source_target_pairs={{1,0},{2,1},{3,2},{4,3},{5,4},{6,5},{7,6},{0,7},{9,8},{10,9},{11,1... | collective-permute-start | bytes 1597448 | tf_op jit(solution)/shard_map/ppermute | solution.py:50
  36.3 2.2 %collective-permute-done = f32[27,1,8,512]{3,2,1,0:T(8,128)} collective-permute-done((f32[27,1,8,512]{3,2,1,0:T(8,128)}, f32[27,1,8,512]{3,2,1,0:T(8,128)}, u32[]{:S(2)}, u32[]{:S(2)}) %collective-permute-start) | collective-permute-done | bytes 442400 | tf_op jit(solution)/shard_map/ppermute | solution.py:47
  38.5 8.1 %collective-permute-done.1 = f32[27,1,8,512]{3,2,1,0:T(8,128)} collective-permute-done((f32[27,1,8,512]{3,2,1,0:T(8,128)}, f32[27,1,8,512]{3,2,1,0:T(8,128)}, u32[]{:S(2)}, u32[]{:S(2)}) %collective-permute-start.1) | collective-permute-done | bytes 442400 | tf_op jit(solution)/shard_map/ppermute | solution.py:50
  46.6 2.2 %pad_maximum_fusion.4 = (f32[27,10,1,512]{3,2,1,0:T(1,128)S(1)}, f32[27,10,1,512]{3,2,1,0:T(1,128)S(1)}) fusion(f32[27,1,8,512]{3,2,1,0:T(8,128)} %collective-permute-done.1, f32[27,1,8,512]{3,2,1,0:T(8,128)} %collective-permute-done, f32[1,8,8,512]{3,2,1,0:T(8,128)S(1)} %copy-done.9, f32[7,8,8,512]{3,2,1,0:T(8,128)S(1)} %fusion.21, ...), kind=kLoop, calls=%fused_computation.71 | loop fusion | flops 1105920 | bytes 5529600 | tf_op jit(solution)/shard_map/slice | solution.py:48
  48.8 2.6 %collective-permute-start.3 = (f32[27,10,1,512]{3,2,1,0:T(1,128)S(1)}, f32[27,10,1,512]{3,2,1,0:T(1,128)S(1)}, u32[]{:S(2)}, u32[]{:S(2)}) collective-permute-start(f32[27,10,1,512]{3,2,1,0:T(1,128)S(1)} %get-tuple-element.103), channel_id=1, source_target_pairs={{1,0},{2,1},{3,2},{4,3},{5,4},{6,5},{7,6},{0,7},{9,8},{10,9},{11,1... | collective-permute-start | bytes 1658888 | tf_op jit(solution)/shard_map/ppermute | solution.py:50
  51.5 13.1 %select_maximum_fusion.6 = f32[26,10,10,514]{3,2,1,0:T(8,128)S(1)} fusion(f32[26,10,1,512]{3,2,1,0:T(1,128)S(1)} %collective-permute-done.6, f32[26,10,1,512]{3,2,1,0:T(1,128)S(1)} %collective-permute-done.7, f32[26,1,8,512]{3,2,1,0:T(8,128)} %collective-permute-done.4, f32[26,8,8,512]{3,2,1,0:T(8,128)S(1)} %copy-done.3, ...), kind=kLoop, calls=%fused_computation.11 | loop fusion | flops 16036800 | bytes 10670400 | tf_op jit(solution)/shard_map/concatenate | solution.py:51
  64.6 21.7 %select_maximum_fusion = f32[27,10,10,514]{3,2,1,0:T(8,128)S(1)} fusion(f32[27,10,1,512]{3,2,1,0:T(1,128)S(1)} %collective-permute-done.3, f32[27,10,1,512]{3,2,1,0:T(1,128)S(1)} %collective-permute-done.2, f32[27,1,8,512]{3,2,1,0:T(8,128)} %collective-permute-done.1, f32[27,1,8,512]{3,2,1,0:T(8,128)} %collective-permute-done, ...), kind=kLoop, calls=%fused_computation.4 | loop fusion | flops 22204800 | bytes 11080800 | tf_op jit(solution)/shard_map/concatenate | solution.py:51
  86.5 0.8 constant_dynamic-update-slice_fusion.64
  87.4 0.8 constant_dynamic-update-slice_fusion.63
  88.2 0.9 constant_dynamic-update-slice_fusion.71
  89.1 0.9 constant_dynamic-update-slice_fusion.70
  89.9 0.1 constant_dynamic-update-slice_fusion.60
  90.1 0.9 constant_dynamic-update-slice_fusion.69
  91.0 0.9 constant_dynamic-update-slice_fusion.68
  91.9 0.8 constant_dynamic-update-slice_fusion.56
  92.7 0.8 constant_dynamic-update-slice_fusion.55
  93.6 0.1 constant_dynamic-update-slice_fusion.54
  93.9 0.1 constant_dynamic-update-slice_fusion.51
  94.2 0.1 constant_dynamic-update-slice_fusion.67
  94.3 0.2 constant_dynamic-update-slice_fusion.66
  94.5 0.4 negate_add_fusion
  94.9 0.2 fusion.255
  95.2 1.0 constant_dynamic-update-slice_fusion.43
  96.1 0.9 constant_dynamic-update-slice_fusion.42
  97.0 0.2 constant_dynamic-update-slice_fusion.41
  97.2 0.2 constant_dynamic-update-slice_fusion.40
  97.5 0.8 constant_dynamic-update-slice_fusion.30
  98.4 0.8 constant_dynamic-update-slice_fusion.29
  99.2 0.8 constant_dynamic-update-slice_fusion.28
  100.1 0.8 constant_dynamic-update-slice_fusion.27
  101.7 0.1 constant_dynamic-update-slice_fusion.38
  101.9 0.2 multiply_reduce_fusion.15
  102.0 0.8 multiply_reduce_fusion
  102.9 0.6 multiply_subtract_fusion.1
  103.7 0.2 copy-done.16
  103.9 0.3 add_multiply_fusion
  104.4 2.6 %fusion.7 = (f32[19,8,8,512]{3,2,1,0:T(8,128)S(1)}, f32[19,8,8,512]{3,2,1,0:T(8,128)S(1)}) fusion(f32[8,8,512]{2,1,0:T(8,128)S(1)} %get-tuple-element.47, f32[8,8,512]{2,1,0:T(8,128)S(1)} %get-tuple-element.40, f32[8,8,512]{2,1,0:T(8,128)S(1)} %get-tuple-element.43, f32[8,8,512]{2,1,0:T(8,128)S(1)} %get-tuple-element.41, f32[19]{0:T(128)S(1)} %copy-done.44, ...), kind=kLoop, calls=%fused_computation.25 | loop fusion | flops 25526272 | bytes 10355011 | tf_op jit(solution)/shard_map/transpose(jvp())/add_any | solution.py:82
  107.1 3.1 %multiply_reduce_fusion.3 = (f32[8,8,512]{2,1,0:T(8,128)}, f32[8,8,512]{2,1,0:T(8,128)S(1)}, f32[8,8,512]{2,1,0:T(8,128)}, f32[8,8,512]{2,1,0:T(8,128)S(1)}, f32[8,8,512]{2,1,0:T(8,128)}) fusion(f32[19,8,8,512]{3,2,1,0:T(8,128)S(1)} %get-tuple-element.48, f32[19]{0:T(128)S(1)} %copy-done.44, f32[19]{0:T(128)S(1)} %copy-done.46, f32[19]{0:T(128)S(1)} %copy-done.45, ...), kind=kLoop, calls=%fused_computation.39 | loop fusion | flops 14778368 | bytes 6291760 | tf_op jit(solution)/shard_map/transpose(jvp())/reduce_sum | solution.py:80
  110.3 1.6 multiply_reduce_fusion.11
  111.9 0.7 multiply_bitcast_fusion
  112.6 5.1 %fusion.18 = f32[32]{0:T(128)} fusion(pred[32,8,8,512]{3,2,1,0:T(8,128)(4,1)S(1)} %copy-done.35, f32[8,8,512,1]{2,1,0,3:T(8,128)S(1)} %get-tuple-element.33), kind=kOutput, calls=%fused_computation.55 | convolution fusion | flops 12582912 | bytes 1179776 | tf_op jit(solution)/shard_map/dot_general | solution.py:159
  117.7 39.0 %psum.7 = f32[32]{0:T(128)} all-reduce(f32[32]{0:T(128)} %fusion.18), channel_id=1, replica_groups=mesh['gx'=4,'gy'=8] {'gx','gy'}, use_global_device_ids=true, to_apply=%region_23.24 | all-reduce | flops 32 | bytes 256 | tf_op jit(solution)/shard_map/psum | solution.py:160
  156.8 1.2 broadcast_multiply_fusion
  158.0 1.0 multiply_add_fusion.3
  159.1 1.1 multiply_add_fusion.1
  160.2 1.2 fusion.239
  161.5 0.2 fusion.236
  161.8 2.5 %add_add_fusion = f32[19,8,8,512]{3,2,1,0:T(8,128)} fusion(f32[19,8,8,512]{3,2,1,0:T(8,128)S(1)} %copy-done.6, f32[19,8,8,512]{3,2,1,0:T(8,128)S(1)} %get-tuple-element.49, f32[8,8,512]{2,1,0:T(8,128)S(1)} %get-tuple-element.133, f32[8,8,512]{2,1,0:T(8,128)S(1)} %get-tuple-element.138, f32[8,8,512]{2,1,0:T(8,128)S(1)} %get-tuple-element.37, ...), kind=kLoop, calls=%fused_computation.36 | loop fusion | flops 6225920 | bytes 8126768 | tf_op jit(solution)/shard_map/transpose(jvp())/add_any | solution.py:68
  (178 shorter events, 2.6 us)
Async XLA Ops:
  0.6 9.1 %copy-start = (f32[32]{0:T(128)S(1)}, f32[32]{0:T(128)}, u32[]{:S(2)}) copy-start(f32[32]{0:T(128)} %param.23) | copy-start | bytes 388
  0.6 2.0 %copy-start.18 = (f32[7,8,8,512]{3,2,1,0:T(8,128)S(1)}, f32[7,8,8,512]{3,2,1,0:T(8,128)}, u32[]{:S(2)}) copy-start(f32[7,8,8,512]{3,2,1,0:T(8,128)} %param.21) | copy-start | bytes 2752516
  2.7 6.2 %copy-start.43 = (s32[8,8,512]{2,1,0:T(8,128)S(1)}, s32[8,8,512]{2,1,0:T(8,128)}, u32[]{:S(2)}) copy-start(s32[8,8,512]{2,1,0:T(8,128)} %param.25) | copy-start | bytes 393220
  2.7 6.8 %copy-start.36 = (f32[7,8,8,512]{3,2,1,0:T(8,128)S(1)}, f32[7,8,8,512]{3,2,1,0:T(8,128)}, u32[]{:S(2)}) copy-start(f32[7,8,8,512]{3,2,1,0:T(8,128)} %param.19) | copy-start | bytes 2752516
  2.7 6.8 %copy-start.47 = (f32[7]{0:T(128)S(1)}, f32[7]{0:T(128)}, u32[]{:S(2)}) copy-start(f32[7]{0:T(128)} %constant.97) | copy-start | bytes 88
  2.8 8.5 %copy-start.2 = (f32[26,8,8,512]{3,2,1,0:T(8,128)}, f32[26,8,8,512]{3,2,1,0:T(8,128)S(1)}, u32[]{:S(2)}) copy-start(f32[26,8,8,512]{3,2,1,0:T(8,128)S(1)} %constant_dynamic-update-slice_fusion.45) | copy-start | bytes 10223620
  3.8 18.4 %collective-permute-start.5 = (f32[26,1,8,512]{3,2,1,0:T(8,128)}, f32[26,1,8,512]{3,2,1,0:T(8,128)}, u32[]{:S(2)}, u32[]{:S(2)}) collective-permute-start(f32[26,1,8,512]{3,2,1,0:T(8,128)} %get-tuple-element.112), channel_id=1, source_target_pairs={{0,8},{8,16},{16,24},{24,0},{1,9},{9,17},{17,25},{25,1},{2,10},{10... | collective-permute-start | bytes 1277960 | tf_op jit(solution)/shard_map/ppermute | solution.py:47
  6.8 4.5 %copy-start.7 = (f32[19,8,8,512]{3,2,1,0:T(8,128)S(1)}, f32[19,8,8,512]{3,2,1,0:T(8,128)}, u32[]{:S(2)}) copy-start(f32[19,8,8,512]{3,2,1,0:T(8,128)} %param.18) | copy-start | bytes 7471108
  6.8 4.5 %copy-start.44 = (f32[19]{0:T(128)S(1)}, f32[19]{0:T(128)}, u32[]{:S(2)}) copy-start(f32[19]{0:T(128)} %constant.54.clone) | copy-start | bytes 232
  6.8 4.5 %copy-start.45 = (f32[19]{0:T(128)S(1)}, f32[19]{0:T(128)}, u32[]{:S(2)}) copy-start(f32[19]{0:T(128)} %constant.53.clone) | copy-start | bytes 232
  6.8 4.5 %copy-start.46 = (f32[19]{0:T(128)S(1)}, f32[19]{0:T(128)}, u32[]{:S(2)}) copy-start(f32[19]{0:T(128)} %constant.52.clone) | copy-start | bytes 232
  6.8 4.5 %copy-start.51 = (f32[19]{0:T(128)S(1)}, f32[19]{0:T(128)}, u32[]{:S(2)}) copy-start(f32[19]{0:T(128)} %constant.101) | copy-start | bytes 232
  6.8 22.3 %collective-permute-start.4 = (f32[26,1,8,512]{3,2,1,0:T(8,128)}, f32[26,1,8,512]{3,2,1,0:T(8,128)}, u32[]{:S(2)}, u32[]{:S(2)}) collective-permute-start(f32[26,1,8,512]{3,2,1,0:T(8,128)} %get-tuple-element.113), channel_id=1, source_target_pairs={{8,0},{16,8},{24,16},{0,24},{9,1},{17,9},{25,17},{1,25},{10,2},{18... | collective-permute-start | bytes 1277960 | tf_op jit(solution)/shard_map/ppermute | solution.py:50
  9.5 2.8 %copy-start.34 = (pred[32,8,8,512]{3,2,1,0:T(8,128)(4,1)}, pred[32,8,8,512]{3,2,1,0:T(8,128)(4,1)S(1)}, u32[]{:S(2)}) copy-start(pred[32,8,8,512]{3,2,1,0:T(8,128)(4,1)S(1)} %iota_compare_fusion.4) | copy-start | bytes 3145732
  9.7 2.6 %copy-start.4 = (s32[8,8,512]{2,1,0:T(8,128)S(1)}, s32[8,8,512]{2,1,0:T(8,128)}, u32[]{:S(2)}) copy-start(s32[8,8,512]{2,1,0:T(8,128)} %param.24) | copy-start | bytes 393220
  11.4 1.2 copy-start.49
  12.6 3.6 %copy-start.15 = (f32[8,8,512]{2,1,0:T(8,128)}, f32[8,8,512]{2,1,0:T(8,128)S(1)}, u32[]{:S(2)}) copy-start(f32[8,8,512]{2,1,0:T(8,128)S(1)} %get-tuple-element.79) | copy-start | bytes 393220
  14.3 1.9 %copy-start.54 = (f32[7]{0:T(128)S(1)}, f32[7]{0:T(128)}, u32[]{:S(2)}) copy-start(f32[7]{0:T(128)} %constant.100) | copy-start | bytes 88
  14.3 1.9 %copy-start.56 = (f32[7]{0:T(128)S(1)}, f32[7]{0:T(128)}, u32[]{:S(2)}) copy-start(f32[7]{0:T(128)} %constant.99) | copy-start | bytes 88
  14.3 1.9 %copy-start.58 = (f32[7]{0:T(128)S(1)}, f32[7]{0:T(128)}, u32[]{:S(2)}) copy-start(f32[7]{0:T(128)} %constant.98) | copy-start | bytes 88
  14.3 1.9 %copy-start.60 = (f32[7]{0:T(128)S(1)}, f32[7]{0:T(128)}, u32[]{:S(2)}) copy-start(f32[7]{0:T(128)} %constant.56.clone) | copy-start | bytes 88
  18.3 20.2 %collective-permute-start = (f32[27,1,8,512]{3,2,1,0:T(8,128)}, f32[27,1,8,512]{3,2,1,0:T(8,128)}, u32[]{:S(2)}, u32[]{:S(2)}) collective-permute-start(f32[27,1,8,512]{3,2,1,0:T(8,128)} %get-tuple-element.110), channel_id=1, source_target_pairs={{0,8},{8,16},{16,24},{24,0},{1,9},{9,17},{17,25},{25,1},{2,10},{10... | collective-permute-start | bytes 1327112 | tf_op jit(solution)/shard_map/ppermute | solution.py:47
  18.3 28.2 %collective-permute-start.1 = (f32[27,1,8,512]{3,2,1,0:T(8,128)}, f32[27,1,8,512]{3,2,1,0:T(8,128)}, u32[]{:S(2)}, u32[]{:S(2)}) collective-permute-start(f32[27,1,8,512]{3,2,1,0:T(8,128)} %get-tuple-element.111), channel_id=1, source_target_pairs={{8,0},{16,8},{24,16},{0,24},{9,1},{17,9},{25,17},{1,25},{10,2},{18... | collective-permute-start | bytes 1327112 | tf_op jit(solution)/shard_map/ppermute | solution.py:50
  22.1 24.4 %copy-start.9 = (f32[1,8,8,512]{3,2,1,0:T(8,128)S(1)}, f32[1,8,8,512]{3,2,1,0:T(8,128)}, u32[]{:S(2)}) copy-start(f32[1,8,8,512]{3,2,1,0:T(8,128)} %copy-done.8) | copy-start | bytes 393220
  33.6 17.9 %collective-permute-start.7 = (f32[26,10,1,512]{3,2,1,0:T(1,128)S(1)}, f32[26,10,1,512]{3,2,1,0:T(1,128)S(1)}, u32[]{:S(2)}, u32[]{:S(2)}) collective-permute-start(f32[26,10,1,512]{3,2,1,0:T(1,128)S(1)} %get-tuple-element.108), channel_id=1, source_target_pairs={{0,1},{1,2},{2,3},{3,4},{4,5},{5,6},{6,7},{7,0},{8,9},{9,10},{10,1... | collective-permute-start | bytes 1597448 | tf_op jit(solution)/shard_map/ppermute | solution.py:47
  33.7 17.8 %collective-permute-start.6 = (f32[26,10,1,512]{3,2,1,0:T(1,128)S(1)}, f32[26,10,1,512]{3,2,1,0:T(1,128)S(1)}, u32[]{:S(2)}, u32[]{:S(2)}) collective-permute-start(f32[26,10,1,512]{3,2,1,0:T(1,128)S(1)} %get-tuple-element.109), channel_id=1, source_target_pairs={{1,0},{2,1},{3,2},{4,3},{5,4},{6,5},{7,6},{0,7},{9,8},{10,9},{11,1... | collective-permute-start | bytes 1597448 | tf_op jit(solution)/shard_map/ppermute | solution.py:50
  36.3 15.2 %copy-start.3 = (f32[26,8,8,512]{3,2,1,0:T(8,128)S(1)}, f32[26,8,8,512]{3,2,1,0:T(8,128)}, u32[]{:S(2)}) copy-start(f32[26,8,8,512]{3,2,1,0:T(8,128)} %copy-done.2) | copy-start | bytes 10223620
  48.8 15.8 %collective-permute-start.2 = (f32[27,10,1,512]{3,2,1,0:T(1,128)S(1)}, f32[27,10,1,512]{3,2,1,0:T(1,128)S(1)}, u32[]{:S(2)}, u32[]{:S(2)}) collective-permute-start(f32[27,10,1,512]{3,2,1,0:T(1,128)S(1)} %get-tuple-element.102), channel_id=1, source_target_pairs={{0,1},{1,2},{2,3},{3,4},{4,5},{5,6},{6,7},{7,0},{8,9},{9,10},{10,1... | collective-permute-start | bytes 1658888 | tf_op jit(solution)/shard_map/ppermute | solution.py:47
  48.8 15.7 %collective-permute-start.3 = (f32[27,10,1,512]{3,2,1,0:T(1,128)S(1)}, f32[27,10,1,512]{3,2,1,0:T(1,128)S(1)}, u32[]{:S(2)}, u32[]{:S(2)}) collective-permute-start(f32[27,10,1,512]{3,2,1,0:T(1,128)S(1)} %get-tuple-element.103), channel_id=1, source_target_pairs={{1,0},{2,1},{3,2},{4,3},{5,4},{6,5},{7,6},{0,7},{9,8},{10,9},{11,1... | collective-permute-start | bytes 1658888 | tf_op jit(solution)/shard_map/ppermute | solution.py:50
  64.5 21.9 %copy-start.10 = (f32[19,8,8,512]{3,2,1,0:T(8,128)S(1)}, f32[19,8,8,512]{3,2,1,0:T(8,128)}, u32[]{:S(2)}) copy-start(f32[19,8,8,512]{3,2,1,0:T(8,128)} %param.20) | copy-start | bytes 7471108
  64.5 21.9 %copy-start.19 = (f32[7,8,8,512]{3,2,1,0:T(8,128)S(1)}, f32[7,8,8,512]{3,2,1,0:T(8,128)}, u32[]{:S(2)}) copy-start(f32[7,8,8,512]{3,2,1,0:T(8,128)} %param.21) | copy-start | bytes 2752516
  94.5 9.7 %copy-start.5 = (f32[19,8,8,512]{3,2,1,0:T(8,128)}, f32[19,8,8,512]{3,2,1,0:T(8,128)S(1)}, u32[]{:S(2)}) copy-start(f32[19,8,8,512]{3,2,1,0:T(8,128)S(1)} %get-tuple-element.87) | copy-start | bytes 7471108
  101.8 1.7 %copy-start.24 = (f32[19,8,8,512]{3,2,1,0:T(8,128)}, f32[19,8,8,512]{3,2,1,0:T(8,128)S(1)}, u32[]{:S(2)}) copy-start(f32[19,8,8,512]{3,2,1,0:T(8,128)S(1)} %get-tuple-element.83) | copy-start | bytes 7471108
  101.8 1.7 %copy-start.25 = (f32[7,8,8,512]{3,2,1,0:T(8,128)}, f32[7,8,8,512]{3,2,1,0:T(8,128)S(1)}, u32[]{:S(2)}) copy-start(f32[7,8,8,512]{3,2,1,0:T(8,128)S(1)} %get-tuple-element.82) | copy-start | bytes 2752516
  103.6 6.6 %copy-start.11 = (f32[8,8,512]{2,1,0:T(8,128)}, f32[8,8,512]{2,1,0:T(8,128)S(1)}, u32[]{:S(2)}) copy-start(f32[8,8,512]{2,1,0:T(8,128)S(1)} %get-tuple-element.40) | copy-start | bytes 393220
  103.6 8.3 %copy-start.13 = (f32[8,8,512]{2,1,0:T(8,128)}, f32[8,8,512]{2,1,0:T(8,128)S(1)}, u32[]{:S(2)}) copy-start(f32[8,8,512]{2,1,0:T(8,128)S(1)} %get-tuple-element.41) | copy-start | bytes 393220
  104.2 5.9 %copy-start.20 = (f32[8,8,512]{2,1,0:T(8,128)}, f32[8,8,512]{2,1,0:T(8,128)S(1)}, u32[]{:S(2)}) copy-start(f32[8,8,512]{2,1,0:T(8,128)S(1)} %get-tuple-element.47) | copy-start | bytes 393220
  104.2 5.9 %copy-start.33 = (f32[8,8,512]{2,1,0:T(8,128)}, f32[8,8,512]{2,1,0:T(8,128)S(1)}, u32[]{:S(2)}) copy-start(f32[8,8,512]{2,1,0:T(8,128)S(1)} %get-tuple-element.45) | copy-start | bytes 393220
  104.3 7.6 %copy-start.30 = (f32[8,8,512]{2,1,0:T(8,128)}, f32[8,8,512]{2,1,0:T(8,128)S(1)}, u32[]{:S(2)}) copy-start(f32[8,8,512]{2,1,0:T(8,128)S(1)} %get-tuple-element.44) | copy-start | bytes 393220
  107.0 3.2 %copy-start.55 = (f32[7]{0:T(128)S(1)}, f32[7]{0:T(128)}, u32[]{:S(2)}) copy-start(f32[7]{0:T(128)} %constant.100) | copy-start | bytes 88
  107.0 3.2 %copy-start.57 = (f32[7]{0:T(128)S(1)}, f32[7]{0:T(128)}, u32[]{:S(2)}) copy-start(f32[7]{0:T(128)} %constant.99) | copy-start | bytes 88
  107.0 3.2 %copy-start.59 = (f32[7]{0:T(128)S(1)}, f32[7]{0:T(128)}, u32[]{:S(2)}) copy-start(f32[7]{0:T(128)} %constant.98) | copy-start | bytes 88
  107.0 3.2 %copy-start.61 = (f32[7]{0:T(128)S(1)}, f32[7]{0:T(128)}, u32[]{:S(2)}) copy-start(f32[7]{0:T(128)} %constant.56.clone) | copy-start | bytes 88
  107.1 3.2 %copy-start.62 = (f32[7]{0:T(128)S(1)}, f32[7]{0:T(128)}, u32[]{:S(2)}) copy-start(f32[7]{0:T(128)} %constant.104) | copy-start | bytes 88
  107.1 3.2 %copy-start.63 = (f32[7]{0:T(128)S(1)}, f32[7]{0:T(128)}, u32[]{:S(2)}) copy-start(f32[7]{0:T(128)} %constant.103) | copy-start | bytes 88
  107.1 3.2 %copy-start.64 = (f32[7]{0:T(128)S(1)}, f32[7]{0:T(128)}, u32[]{:S(2)}) copy-start(f32[7]{0:T(128)} %constant.102) | copy-start | bytes 88
  110.2 1.7 %copy-start.42 = (f32[8,8,512]{2,1,0:T(8,128)S(1)}, f32[8,8,512]{2,1,0:T(8,128)}, u32[]{:S(2)}) copy-start(f32[8,8,512]{2,1,0:T(8,128)} %param.22) | copy-start | bytes 393220
  110.2 2.4 %copy-start.35 = (pred[32,8,8,512]{3,2,1,0:T(8,128)(4,1)S(1)}, pred[32,8,8,512]{3,2,1,0:T(8,128)(4,1)}, u32[]{:S(2)}) copy-start(pred[32,8,8,512]{3,2,1,0:T(8,128)(4,1)} %copy-done.34) | copy-start | bytes 3145732
  111.9 46.2 %copy-start.12 = (f32[8,8,512]{2,1,0:T(8,128)S(1)}, f32[8,8,512]{2,1,0:T(8,128)}, u32[]{:S(2)}) copy-start(f32[8,8,512]{2,1,0:T(8,128)} %copy-done.11) | copy-start | bytes 393220
  111.9 46.2 %copy-start.17 = (f32[8,8,512]{2,1,0:T(8,128)S(1)}, f32[8,8,512]{2,1,0:T(8,128)}, u32[]{:S(2)}) copy-start(f32[8,8,512]{2,1,0:T(8,128)} %copy-done.15) | copy-start | bytes 393220
  112.6 45.4 %copy-start.14 = (f32[8,8,512]{2,1,0:T(8,128)S(1)}, f32[8,8,512]{2,1,0:T(8,128)}, u32[]{:S(2)}) copy-start(f32[8,8,512]{2,1,0:T(8,128)} %copy-done.13) | copy-start | bytes 393220
  112.6 47.6 %copy-start.23 = (f32[8,8,512]{2,1,0:T(8,128)S(1)}, f32[8,8,512]{2,1,0:T(8,128)}, u32[]{:S(2)}) copy-start(f32[8,8,512]{2,1,0:T(8,128)} %copy-done.22) | copy-start | bytes 393220
  117.7 43.7 %copy-start.21 = (f32[8,8,512]{2,1,0:T(8,128)S(1)}, f32[8,8,512]{2,1,0:T(8,128)}, u32[]{:S(2)}) copy-start(f32[8,8,512]{2,1,0:T(8,128)} %copy-done.20) | copy-start | bytes 393220
  117.7 43.7 %copy-start.27 = (f32[8,8,512]{2,1,0:T(8,128)S(1)}, f32[8,8,512]{2,1,0:T(8,128)}, u32[]{:S(2)}) copy-start(f32[8,8,512]{2,1,0:T(8,128)} %copy-done.26) | copy-start | bytes 393220
  156.7 4.7 %copy-start.29 = (f32[8,8,512]{2,1,0:T(8,128)S(1)}, f32[8,8,512]{2,1,0:T(8,128)}, u32[]{:S(2)}) copy-start(f32[8,8,512]{2,1,0:T(8,128)} %copy-done.28) | copy-start | bytes 393220
  156.7 4.7 %copy-start.31 = (f32[8,8,512]{2,1,0:T(8,128)S(1)}, f32[8,8,512]{2,1,0:T(8,128)}, u32[]{:S(2)}) copy-start(f32[8,8,512]{2,1,0:T(8,128)} %copy-done.30) | copy-start | bytes 393220
  156.7 4.7 %copy-start.32 = (f32[8,8,512]{2,1,0:T(8,128)S(1)}, f32[8,8,512]{2,1,0:T(8,128)}, u32[]{:S(2)}) copy-start(f32[8,8,512]{2,1,0:T(8,128)} %get-tuple-element.34) | copy-start | bytes 393220
  156.8 4.7 %copy-start.37 = (f32[8,8,512]{2,1,0:T(8,128)S(1)}, f32[8,8,512]{2,1,0:T(8,128)}, u32[]{:S(2)}) copy-start(f32[8,8,512]{2,1,0:T(8,128)} %get-tuple-element.11) | copy-start | bytes 393220
  156.8 4.7 %copy-start.38 = (f32[8,8,512]{2,1,0:T(8,128)S(1)}, f32[8,8,512]{2,1,0:T(8,128)}, u32[]{:S(2)}) copy-start(f32[8,8,512]{2,1,0:T(8,128)} %get-tuple-element.32) | copy-start | bytes 393220
  156.8 4.7 %copy-start.39 = (f32[8,8,512]{2,1,0:T(8,128)S(1)}, f32[8,8,512]{2,1,0:T(8,128)}, u32[]{:S(2)}) copy-start(f32[8,8,512]{2,1,0:T(8,128)} %get-tuple-element.26) | copy-start | bytes 393220
  156.8 4.7 %copy-start.40 = (f32[8,8,512]{2,1,0:T(8,128)S(1)}, f32[8,8,512]{2,1,0:T(8,128)}, u32[]{:S(2)}) copy-start(f32[8,8,512]{2,1,0:T(8,128)} %get-tuple-element.28) | copy-start | bytes 393220
  159.1 2.6 %copy-start.6 = (f32[19,8,8,512]{3,2,1,0:T(8,128)S(1)}, f32[19,8,8,512]{3,2,1,0:T(8,128)}, u32[]{:S(2)}) copy-start(f32[19,8,8,512]{3,2,1,0:T(8,128)} %copy-done.5) | copy-start | bytes 7471108
  159.1 2.6 %copy-start.53 = (f32[19]{0:T(128)S(1)}, f32[19]{0:T(128)}, u32[]{:S(2)}) copy-start(f32[19]{0:T(128)} %constant.101) | copy-start | bytes 232
  161.7 2.6 %copy-start.1 = (f32[32]{0:T(128)S(1)}, f32[32]{0:T(128)}, u32[]{:S(2)}) copy-start(f32[32]{0:T(128)} %param.23) | copy-start | bytes 388
  (10 other events, 8.0 us)
where the time goes:
time: 167 us; the launch traced here: 164 us
  other arithmetic  80.1 us (48%)
  blocking collectives  39 us (23%)
  waiting for transfers between devices  17.2 us (10%)
  starting transfers between devices  14.3 us (9%)
  matrix products  6.66 us (4%)
  local copies, waits for them, and re-layouts  4.91 us (3%)
  between operations  1.99 us (1%)
    concatenate x3, other arithmetic, with_halo(): block = jnp.concatenate([low, block, high], axis=dim)  39.2 us
    psum x1, blocking collectives, on_device(): totals = lax.psum(shares, ('gx', 'gy'))  39 us
    ppermute x4, waiting for transfers between devices, with_halo(): lax.ppermute(lax.slice_in_dim(block, 0, width, axis=dim), axis, backward)  15.1 us
    unnamed x35, other arithmetic  14.2 us
    ppermute x4, starting transfers between devices, with_halo(): lax.ppermute(lax.slice_in_dim(block, 0, width, axis=dim), axis, backward)  11.2 us
    dot_general x1, matrix products, on_device(): jnp.tensordot(table, dcell * profile, axes=3, precision=lax.Precision.HIG...  5.09 us
    unnamed x151, local copies, waits for them, and re-layouts  3.65 us
  transfers between devices with their start and end apart: 8, of which 3 were waited for; matrix products, arithmetic and copies ran while one was open for 17% of the time, Pallas kernels for 0%

commit v1 on v0

--- a/solution.py
+++ b/solution.py
@@ -157,7 +157,9 @@
     _, pullback = jax.vjp(local_collide, new_flow, new_field, bcell)
     adj_flow, adj_field, dcell = pullback((ast_flow, ast_field))
     shares = jnp.tensordot(table, dcell * profile, axes=3, precision=lax.Precision.HIGHEST)
-    totals = lax.psum(shares, ("gx", "gy"))
+    totals = shares
+    for j in ("gy", "gx"):
+        totals = lax.psum(totals, axis_name=j)
     cells = (
         flow.shape[1] * lax.axis_size("gx") * flow.shape[2] * lax.axis_size("gy") * flow.shape[3]
     )

time: 167 us -> 152 us (0.910)
  blocking collectives: 39 us -> 24.6 us
    psum x1 -> x2, blocking collectives: 39 us -> 24.6 us  [on_device(): totals = lax.psum(totals, axis_name=j)]
  transfers between devices with their start and end apart: 8 -> 8, of which waited for: 3 -> 3; matrix products, arithmetic and copies ran while one was open for 17% -> 19% of each run, Pallas kernels for 0% -> 0%
where the time goes in v1:
time: 152 us; the launch traced here: 150 us
  other arithmetic  80.2 us (53%)
  blocking collectives  24.6 us (16%)
  waiting for transfers between devices  17.2 us (11%)
  starting transfers between devices  14.3 us (9%)
  matrix products  6.66 us (4%)
  local copies, waits for them, and re-layouts  4.92 us (3%)
  between operations  1.98 us (1%)
    concatenate x3, other arithmetic, with_halo(): block = jnp.concatenate([low, block, high], axis=dim)  39.3 us
    psum x2, blocking collectives, on_device(): totals = lax.psum(totals, axis_name=j)  24.6 us
    ppermute x4, waiting for transfers between devices, with_halo(): lax.ppermute(lax.slice_in_dim(block, 0, width, axis=dim), axis, backward)  15 us
    unnamed x35, other arithmetic  14.2 us
    ppermute x4, starting transfers between devices, with_halo(): lax.ppermute(lax.slice_in_dim(block, 0, width, axis=dim), axis, backward)  11.2 us
    dot_general x1, matrix products, on_device(): jnp.tensordot(table, dcell * profile, axes=3, precision=lax.Precision.HIG...  5.09 us
    unnamed x151, local copies, waits for them, and re-layouts  3.66 us
    slice x2, other arithmetic, with_halo(): lax.slice_in_dim(block, block.shape[dim] - width, None, axis=dim)  3.17 us
  transfers between devices with their start and end apart: 8, of which 3 were waited for; matrix products, arithmetic and copies ran while one was open for 19% of the time, Pallas kernels for 0%

profile of v1, /device:TPU:0, one launch (start us, length us, event | category | flops | bytes accessed | tf_op | source)
XLA Modules:
  0.0 149.9 jit_solution(9207649444324201465)
XLA Ops:
  0.7 2.0 %constant_dynamic-update-slice_fusion.46 = f32[26,8,8,512]{3,2,1,0:T(8,128)S(1)} fusion(f32[19,8,8,512]{3,2,1,0:T(8,128)} %param.20), kind=kLoop, calls=%fused_computation.129 | loop fusion | bytes 4980736
  2.8 1.0 fusion.254
  3.8 3.0 %collective-permute-start.5 = (f32[26,1,8,512]{3,2,1,0:T(8,128)}, f32[26,1,8,512]{3,2,1,0:T(8,128)}, u32[]{:S(2)}, u32[]{:S(2)}) collective-permute-start(f32[26,1,8,512]{3,2,1,0:T(8,128)} %get-tuple-element.112), channel_id=1, source_target_pairs={{0,8},{8,16},{16,24},{24,0},{1,9},{9,17},{17,25},{25,1},{2,10},{10... | collective-permute-start | bytes 1277960 | tf_op jit(solution)/shard_map/ppermute | solution.py:47
  6.8 2.1 %collective-permute-start.4 = (f32[26,1,8,512]{3,2,1,0:T(8,128)}, f32[26,1,8,512]{3,2,1,0:T(8,128)}, u32[]{:S(2)}, u32[]{:S(2)}) collective-permute-start(f32[26,1,8,512]{3,2,1,0:T(8,128)} %get-tuple-element.113), channel_id=1, source_target_pairs={{8,0},{16,8},{24,16},{0,24},{9,1},{17,9},{25,17},{1,25},{10,2},{18... | collective-permute-start | bytes 1277960 | tf_op jit(solution)/shard_map/ppermute | solution.py:50
  8.9 0.6 iota_compare_fusion.4
  9.6 0.1 fusion.238
  9.7 1.6 %fusion.4 = f32[1,8,8,512]{3,0,2,1:T(1,128)S(1)} fusion(pred[32,8,8,512]{3,2,1,0:T(8,128)(4,1)S(1)} %iota_compare_fusion.4, f32[32]{0:T(128)S(1)} %copy-done), kind=kOutput, calls=%fused_computation.22 | convolution fusion | flops 12582912 | bytes 1179776 | tf_op jit(solution)/shard_map/dot_general | solution.py:141
  11.4 1.0 multiply_reduce_fusion.7
  12.6 1.3 fusion.16
  14.3 1.8 %multiply_subtract_fusion = f32[19,8,8,512]{3,2,1,0:T(8,128)S(1)} fusion(f32[19,8,8,512]{3,2,1,0:T(8,128)S(1)} %constant_dynamic-update-slice_fusion, f32[19,8,8,512]{3,2,1,0:T(8,128)S(1)} %copy-done.7, f32[8,8,512]{2,1,0:T(8,128)S(1)} %get-tuple-element.77, f32[8,8,512]{2,1,0:T(8,128)S(1)} %get-tuple-element.81, f32[19]{0:T(128)S(1)} %copy-done.44, ...), kind=kLoop, calls=%fused_computation.48 | loop fusion | flops 12451840 | bytes 8126768 | tf_op jit(solution)/shard_map/sub | solution.py:86
  16.2 0.4 fusion.21
  16.7 0.7 copy-done.8
  17.3 1.0 pad_maximum_fusion.10
  18.3 3.8 %collective-permute-start.1 = (f32[27,1,8,512]{3,2,1,0:T(8,128)}, f32[27,1,8,512]{3,2,1,0:T(8,128)}, u32[]{:S(2)}, u32[]{:S(2)}) collective-permute-start(f32[27,1,8,512]{3,2,1,0:T(8,128)} %get-tuple-element.111), channel_id=1, source_target_pairs={{8,0},{16,8},{24,16},{0,24},{9,1},{17,9},{25,17},{1,25},{10,2},{18... | collective-permute-start | bytes 1327112 | tf_op jit(solution)/shard_map/ppermute | solution.py:50
  22.1 7.0 %collective-permute-done.4 = f32[26,1,8,512]{3,2,1,0:T(8,128)} collective-permute-done((f32[26,1,8,512]{3,2,1,0:T(8,128)}, f32[26,1,8,512]{3,2,1,0:T(8,128)}, u32[]{:S(2)}, u32[]{:S(2)}) %collective-permute-start.4) | collective-permute-done | bytes 426016 | tf_op jit(solution)/shard_map/ppermute | solution.py:50
  29.1 4.5 %pad_maximum_fusion.5 = (f32[26,10,1,512]{3,2,1,0:T(1,128)S(1)}, f32[26,10,1,512]{3,2,1,0:T(1,128)S(1)}) fusion(f32[26,1,8,512]{3,2,1,0:T(8,128)} %collective-permute-done.4, f32[26,8,8,512]{3,2,1,0:T(8,128)} %copy-done.2, f32[26,1,8,512]{3,2,1,0:T(8,128)} %collective-permute-done.5), kind=kLoop, calls=%fused_computation.72 | loop fusion | flops 532480 | bytes 5324800 | tf_op jit(solution)/shard_map/concatenate | solution.py:51
  33.7 2.6 %collective-permute-start.6 = (f32[26,10,1,512]{3,2,1,0:T(1,128)S(1)}, f32[26,10,1,512]{3,2,1,0:T(1,128)S(1)}, u32[]{:S(2)}, u32[]{:S(2)}) collective-permute-start(f32[26,10,1,512]{3,2,1,0:T(1,128)S(1)} %get-tuple-element.109), channel_id=1, source_target_pairs={{1,0},{2,1},{3,2},{4,3},{5,4},{6,5},{7,6},{0,7},{9,8},{10,9},{11,1... | collective-permute-start | bytes 1597448 | tf_op jit(solution)/shard_map/ppermute | solution.py:50
  36.3 2.2 %collective-permute-done = f32[27,1,8,512]{3,2,1,0:T(8,128)} collective-permute-done((f32[27,1,8,512]{3,2,1,0:T(8,128)}, f32[27,1,8,512]{3,2,1,0:T(8,128)}, u32[]{:S(2)}, u32[]{:S(2)}) %collective-permute-start) | collective-permute-done | bytes 442400 | tf_op jit(solution)/shard_map/ppermute | solution.py:47
  38.5 8.1 %collective-permute-done.1 = f32[27,1,8,512]{3,2,1,0:T(8,128)} collective-permute-done((f32[27,1,8,512]{3,2,1,0:T(8,128)}, f32[27,1,8,512]{3,2,1,0:T(8,128)}, u32[]{:S(2)}, u32[]{:S(2)}) %collective-permute-start.1) | collective-permute-done | bytes 442400 | tf_op jit(solution)/shard_map/ppermute | solution.py:50
  46.6 2.2 %pad_maximum_fusion.4 = (f32[27,10,1,512]{3,2,1,0:T(1,128)S(1)}, f32[27,10,1,512]{3,2,1,0:T(1,128)S(1)}) fusion(f32[27,1,8,512]{3,2,1,0:T(8,128)} %collective-permute-done.1, f32[27,1,8,512]{3,2,1,0:T(8,128)} %collective-permute-done, f32[1,8,8,512]{3,2,1,0:T(8,128)S(1)} %copy-done.9, f32[7,8,8,512]{3,2,1,0:T(8,128)S(1)} %fusion.21, ...), kind=kLoop, calls=%fused_computation.71 | loop fusion | flops 1105920 | bytes 5529600 | tf_op jit(solution)/shard_map/slice | solution.py:48
  48.8 2.6 %collective-permute-start.3 = (f32[27,10,1,512]{3,2,1,0:T(1,128)S(1)}, f32[27,10,1,512]{3,2,1,0:T(1,128)S(1)}, u32[]{:S(2)}, u32[]{:S(2)}) collective-permute-start(f32[27,10,1,512]{3,2,1,0:T(1,128)S(1)} %get-tuple-element.103), channel_id=1, source_target_pairs={{1,0},{2,1},{3,2},{4,3},{5,4},{6,5},{7,6},{0,7},{9,8},{10,9},{11,1... | collective-permute-start | bytes 1658888 | tf_op jit(solution)/shard_map/ppermute | solution.py:50
  51.5 13.1 %select_maximum_fusion.6 = f32[26,10,10,514]{3,2,1,0:T(8,128)S(1)} fusion(f32[26,10,1,512]{3,2,1,0:T(1,128)S(1)} %collective-permute-done.6, f32[26,10,1,512]{3,2,1,0:T(1,128)S(1)} %collective-permute-done.7, f32[26,1,8,512]{3,2,1,0:T(8,128)} %collective-permute-done.4, f32[26,8,8,512]{3,2,1,0:T(8,128)S(1)} %copy-done.3, ...), kind=kLoop, calls=%fused_computation.11 | loop fusion | flops 16036800 | bytes 10670400 | tf_op jit(solution)/shard_map/concatenate | solution.py:51
  64.6 21.7 %select_maximum_fusion = f32[27,10,10,514]{3,2,1,0:T(8,128)S(1)} fusion(f32[27,10,1,512]{3,2,1,0:T(1,128)S(1)} %collective-permute-done.3, f32[27,10,1,512]{3,2,1,0:T(1,128)S(1)} %collective-permute-done.2, f32[27,1,8,512]{3,2,1,0:T(8,128)} %collective-permute-done.1, f32[27,1,8,512]{3,2,1,0:T(8,128)} %collective-permute-done, ...), kind=kLoop, calls=%fused_computation.4 | loop fusion | flops 22204800 | bytes 11080800 | tf_op jit(solution)/shard_map/concatenate | solution.py:51
  86.5 0.8 constant_dynamic-update-slice_fusion.64
  87.4 0.8 constant_dynamic-update-slice_fusion.63
  88.2 0.9 constant_dynamic-update-slice_fusion.71
  89.1 0.9 constant_dynamic-update-slice_fusion.70
  89.9 0.1 constant_dynamic-update-slice_fusion.60
  90.1 0.9 constant_dynamic-update-slice_fusion.69
  91.0 0.9 constant_dynamic-update-slice_fusion.68
  91.9 0.8 constant_dynamic-update-slice_fusion.56
  92.7 0.8 constant_dynamic-update-slice_fusion.55
  93.6 0.1 constant_dynamic-update-slice_fusion.54
  94.2 0.1 constant_dynamic-update-slice_fusion.67
  94.3 0.2 constant_dynamic-update-slice_fusion.66
  94.5 0.4 negate_add_fusion
  94.9 0.2 fusion.255
  95.2 1.0 constant_dynamic-update-slice_fusion.43
  96.1 0.9 constant_dynamic-update-slice_fusion.42
  97.0 0.2 constant_dynamic-update-slice_fusion.41
  97.2 0.2 constant_dynamic-update-slice_fusion.40
  97.5 0.8 constant_dynamic-update-slice_fusion.30
  98.4 0.8 constant_dynamic-update-slice_fusion.29
  99.2 0.8 constant_dynamic-update-slice_fusion.28
  100.1 0.8 constant_dynamic-update-slice_fusion.27
  101.7 0.1 constant_dynamic-update-slice_fusion.38
  101.9 0.2 multiply_reduce_fusion.15
  102.0 0.8 multiply_reduce_fusion
  102.9 0.6 multiply_subtract_fusion.1
  103.7 0.2 copy-done.16
  103.9 0.3 add_multiply_fusion
  104.3 2.6 %fusion.7 = (f32[19,8,8,512]{3,2,1,0:T(8,128)S(1)}, f32[19,8,8,512]{3,2,1,0:T(8,128)S(1)}) fusion(f32[8,8,512]{2,1,0:T(8,128)S(1)} %get-tuple-element.47, f32[8,8,512]{2,1,0:T(8,128)S(1)} %get-tuple-element.40, f32[8,8,512]{2,1,0:T(8,128)S(1)} %get-tuple-element.43, f32[8,8,512]{2,1,0:T(8,128)S(1)} %get-tuple-element.41, f32[19]{0:T(128)S(1)} %copy-done.44, ...), kind=kLoop, calls=%fused_computation.25 | loop fusion | flops 25526272 | bytes 10355011 | tf_op jit(solution)/shard_map/transpose(jvp())/add_any | solution.py:82
  107.1 3.0 %multiply_reduce_fusion.3 = (f32[8,8,512]{2,1,0:T(8,128)}, f32[8,8,512]{2,1,0:T(8,128)S(1)}, f32[8,8,512]{2,1,0:T(8,128)}, f32[8,8,512]{2,1,0:T(8,128)S(1)}, f32[8,8,512]{2,1,0:T(8,128)}) fusion(f32[19,8,8,512]{3,2,1,0:T(8,128)S(1)} %get-tuple-element.48, f32[19]{0:T(128)S(1)} %copy-done.44, f32[19]{0:T(128)S(1)} %copy-done.46, f32[19]{0:T(128)S(1)} %copy-done.45, ...), kind=kLoop, calls=%fused_computation.39 | loop fusion | flops 14778368 | bytes 6291760 | tf_op jit(solution)/shard_map/transpose(jvp())/reduce_sum | solution.py:80
  110.2 1.6 %multiply_reduce_fusion.11 = (f32[8,8,512]{2,1,0:T(8,128)S(1)}, f32[8,8,512]{2,1,0:T(8,128)S(1)}, f32[8,8,512]{2,1,0:T(8,128)}, f32[8,8,512]{2,1,0:T(8,128)}, f32[8,8,512]{2,1,0:T(8,128)}, /*index=5*/f32[8,8,512]{2,1,0:T(8,128)}) fusion(f32[7,8,8,512]{3,2,1,0:T(8,128)S(1)} %get-tuple-element.86, f32[8,8,512]{2,1,0:T(8,128)S(1)} %get-tuple-element.39, ...), kind=kLoop, calls=%fused_computation.58 | loop fusion | flops 5308416 | bytes 2490592 | tf_op jit(solution)/shard_map/transpose(jvp())/reduce_sum | solution.py:89
  111.9 0.7 multiply_bitcast_fusion
  112.6 5.1 %fusion.18 = f32[32]{0:T(128)} fusion(pred[32,8,8,512]{3,2,1,0:T(8,128)(4,1)S(1)} %copy-done.35, f32[8,8,512,1]{2,1,0,3:T(8,128)S(1)} %get-tuple-element.33), kind=kOutput, calls=%fused_computation.55 | convolution fusion | flops 12582912 | bytes 1179776 | tf_op jit(solution)/shard_map/dot_general | solution.py:159
  117.7 13.4 %psum.14 = f32[32]{0:T(128)} all-reduce(f32[32]{0:T(128)} %fusion.18), channel_id=1, replica_groups=mesh['gx'=4,'gy'=8] {'gy'}, use_global_device_ids=true, to_apply=%region_23.24 | all-reduce | flops 32 | bytes 256 | tf_op jit(solution)/shard_map/psum | solution.py:162
  131.1 11.2 %psum.15 = f32[32]{0:T(128)} all-reduce(f32[32]{0:T(128)} %psum.14), channel_id=1, replica_groups=mesh['gx'=4,'gy'=8] {'gx'}, use_global_device_ids=true, to_apply=%region_24.25 | all-reduce | flops 32 | bytes 256 | tf_op jit(solution)/shard_map/psum | solution.py:162
  142.3 1.2 broadcast_multiply_fusion
  143.6 1.0 multiply_add_fusion.3
  144.7 1.1 multiply_add_fusion.1
  145.8 1.2 fusion.239
  147.0 0.2 fusion.236
  147.3 2.5 %add_add_fusion = f32[19,8,8,512]{3,2,1,0:T(8,128)} fusion(f32[19,8,8,512]{3,2,1,0:T(8,128)S(1)} %copy-done.6, f32[19,8,8,512]{3,2,1,0:T(8,128)S(1)} %get-tuple-element.49, f32[8,8,512]{2,1,0:T(8,128)S(1)} %get-tuple-element.133, f32[8,8,512]{2,1,0:T(8,128)S(1)} %get-tuple-element.138, f32[8,8,512]{2,1,0:T(8,128)S(1)} %get-tuple-element.37, ...), kind=kLoop, calls=%fused_computation.36 | loop fusion | flops 6225920 | bytes 8126768 | tf_op jit(solution)/shard_map/transpose(jvp())/add_any | solution.py:68
  (179 shorter events, 2.8 us)
Async XLA Ops:
  0.6 9.1 %copy-start = (f32[32]{0:T(128)S(1)}, f32[32]{0:T(128)}, u32[]{:S(2)}) copy-start(f32[32]{0:T(128)} %param.23) | copy-start | bytes 388
  0.6 2.0 %copy-start.18 = (f32[7,8,8,512]{3,2,1,0:T(8,128)S(1)}, f32[7,8,8,512]{3,2,1,0:T(8,128)}, u32[]{:S(2)}) copy-start(f32[7,8,8,512]{3,2,1,0:T(8,128)} %param.21) | copy-start | bytes 2752516
  2.7 6.2 %copy-start.43 = (s32[8,8,512]{2,1,0:T(8,128)S(1)}, s32[8,8,512]{2,1,0:T(8,128)}, u32[]{:S(2)}) copy-start(s32[8,8,512]{2,1,0:T(8,128)} %param.25) | copy-start | bytes 393220
  2.7 6.8 %copy-start.36 = (f32[7,8,8,512]{3,2,1,0:T(8,128)S(1)}, f32[7,8,8,512]{3,2,1,0:T(8,128)}, u32[]{:S(2)}) copy-start(f32[7,8,8,512]{3,2,1,0:T(8,128)} %param.19) | copy-start | bytes 2752516
  2.7 6.8 %copy-start.47 = (f32[7]{0:T(128)S(1)}, f32[7]{0:T(128)}, u32[]{:S(2)}) copy-start(f32[7]{0:T(128)} %constant.97) | copy-start | bytes 88
  2.8 8.5 %copy-start.2 = (f32[26,8,8,512]{3,2,1,0:T(8,128)}, f32[26,8,8,512]{3,2,1,0:T(8,128)S(1)}, u32[]{:S(2)}) copy-start(f32[26,8,8,512]{3,2,1,0:T(8,128)S(1)} %constant_dynamic-update-slice_fusion.45) | copy-start | bytes 10223620
  3.8 18.4 %collective-permute-start.5 = (f32[26,1,8,512]{3,2,1,0:T(8,128)}, f32[26,1,8,512]{3,2,1,0:T(8,128)}, u32[]{:S(2)}, u32[]{:S(2)}) collective-permute-start(f32[26,1,8,512]{3,2,1,0:T(8,128)} %get-tuple-element.112), channel_id=1, source_target_pairs={{0,8},{8,16},{16,24},{24,0},{1,9},{9,17},{17,25},{25,1},{2,10},{10... | collective-permute-start | bytes 1277960 | tf_op jit(solution)/shard_map/ppermute | solution.py:47
  6.8 4.5 %copy-start.7 = (f32[19,8,8,512]{3,2,1,0:T(8,128)S(1)}, f32[19,8,8,512]{3,2,1,0:T(8,128)}, u32[]{:S(2)}) copy-start(f32[19,8,8,512]{3,2,1,0:T(8,128)} %param.18) | copy-start | bytes 7471108
  6.8 4.5 %copy-start.44 = (f32[19]{0:T(128)S(1)}, f32[19]{0:T(128)}, u32[]{:S(2)}) copy-start(f32[19]{0:T(128)} %constant.54.clone) | copy-start | bytes 232
  6.8 4.5 %copy-start.45 = (f32[19]{0:T(128)S(1)}, f32[19]{0:T(128)}, u32[]{:S(2)}) copy-start(f32[19]{0:T(128)} %constant.53.clone) | copy-start | bytes 232
  6.8 4.5 %copy-start.46 = (f32[19]{0:T(128)S(1)}, f32[19]{0:T(128)}, u32[]{:S(2)}) copy-start(f32[19]{0:T(128)} %constant.52.clone) | copy-start | bytes 232
  6.8 4.5 %copy-start.51 = (f32[19]{0:T(128)S(1)}, f32[19]{0:T(128)}, u32[]{:S(2)}) copy-start(f32[19]{0:T(128)} %constant.101) | copy-start | bytes 232
  6.8 22.3 %collective-permute-start.4 = (f32[26,1,8,512]{3,2,1,0:T(8,128)}, f32[26,1,8,512]{3,2,1,0:T(8,128)}, u32[]{:S(2)}, u32[]{:S(2)}) collective-permute-start(f32[26,1,8,512]{3,2,1,0:T(8,128)} %get-tuple-element.113), channel_id=1, source_target_pairs={{8,0},{16,8},{24,16},{0,24},{9,1},{17,9},{25,17},{1,25},{10,2},{18... | collective-permute-start | bytes 1277960 | tf_op jit(solution)/shard_map/ppermute | solution.py:50
  9.5 2.8 %copy-start.34 = (pred[32,8,8,512]{3,2,1,0:T(8,128)(4,1)}, pred[32,8,8,512]{3,2,1,0:T(8,128)(4,1)S(1)}, u32[]{:S(2)}) copy-start(pred[32,8,8,512]{3,2,1,0:T(8,128)(4,1)S(1)} %iota_compare_fusion.4) | copy-start | bytes 3145732
  9.7 2.6 %copy-start.4 = (s32[8,8,512]{2,1,0:T(8,128)S(1)}, s32[8,8,512]{2,1,0:T(8,128)}, u32[]{:S(2)}) copy-start(s32[8,8,512]{2,1,0:T(8,128)} %param.24) | copy-start | bytes 393220
  11.4 1.2 copy-start.49
  12.6 3.6 %copy-start.15 = (f32[8,8,512]{2,1,0:T(8,128)}, f32[8,8,512]{2,1,0:T(8,128)S(1)}, u32[]{:S(2)}) copy-start(f32[8,8,512]{2,1,0:T(8,128)S(1)} %get-tuple-element.79) | copy-start | bytes 393220
  14.3 1.9 %copy-start.54 = (f32[7]{0:T(128)S(1)}, f32[7]{0:T(128)}, u32[]{:S(2)}) copy-start(f32[7]{0:T(128)} %constant.100) | copy-start | bytes 88
  14.3 1.9 %copy-start.56 = (f32[7]{0:T(128)S(1)}, f32[7]{0:T(128)}, u32[]{:S(2)}) copy-start(f32[7]{0:T(128)} %constant.99) | copy-start | bytes 88
  14.3 1.9 %copy-start.58 = (f32[7]{0:T(128)S(1)}, f32[7]{0:T(128)}, u32[]{:S(2)}) copy-start(f32[7]{0:T(128)} %constant.98) | copy-start | bytes 88
  14.3 1.9 %copy-start.60 = (f32[7]{0:T(128)S(1)}, f32[7]{0:T(128)}, u32[]{:S(2)}) copy-start(f32[7]{0:T(128)} %constant.56.clone) | copy-start | bytes 88
  18.3 20.2 %collective-permute-start = (f32[27,1,8,512]{3,2,1,0:T(8,128)}, f32[27,1,8,512]{3,2,1,0:T(8,128)}, u32[]{:S(2)}, u32[]{:S(2)}) collective-permute-start(f32[27,1,8,512]{3,2,1,0:T(8,128)} %get-tuple-element.110), channel_id=1, source_target_pairs={{0,8},{8,16},{16,24},{24,0},{1,9},{9,17},{17,25},{25,1},{2,10},{10... | collective-permute-start | bytes 1327112 | tf_op jit(solution)/shard_map/ppermute | solution.py:47
  18.3 28.2 %collective-permute-start.1 = (f32[27,1,8,512]{3,2,1,0:T(8,128)}, f32[27,1,8,512]{3,2,1,0:T(8,128)}, u32[]{:S(2)}, u32[]{:S(2)}) collective-permute-start(f32[27,1,8,512]{3,2,1,0:T(8,128)} %get-tuple-element.111), channel_id=1, source_target_pairs={{8,0},{16,8},{24,16},{0,24},{9,1},{17,9},{25,17},{1,25},{10,2},{18... | collective-permute-start | bytes 1327112 | tf_op jit(solution)/shard_map/ppermute | solution.py:50
  22.1 24.4 %copy-start.9 = (f32[1,8,8,512]{3,2,1,0:T(8,128)S(1)}, f32[1,8,8,512]{3,2,1,0:T(8,128)}, u32[]{:S(2)}) copy-start(f32[1,8,8,512]{3,2,1,0:T(8,128)} %copy-done.8) | copy-start | bytes 393220
  33.6 17.8 %collective-permute-start.7 = (f32[26,10,1,512]{3,2,1,0:T(1,128)S(1)}, f32[26,10,1,512]{3,2,1,0:T(1,128)S(1)}, u32[]{:S(2)}, u32[]{:S(2)}) collective-permute-start(f32[26,10,1,512]{3,2,1,0:T(1,128)S(1)} %get-tuple-element.108), channel_id=1, source_target_pairs={{0,1},{1,2},{2,3},{3,4},{4,5},{5,6},{6,7},{7,0},{8,9},{9,10},{10,1... | collective-permute-start | bytes 1597448 | tf_op jit(solution)/shard_map/ppermute | solution.py:47
  33.7 17.8 %collective-permute-start.6 = (f32[26,10,1,512]{3,2,1,0:T(1,128)S(1)}, f32[26,10,1,512]{3,2,1,0:T(1,128)S(1)}, u32[]{:S(2)}, u32[]{:S(2)}) collective-permute-start(f32[26,10,1,512]{3,2,1,0:T(1,128)S(1)} %get-tuple-element.109), channel_id=1, source_target_pairs={{1,0},{2,1},{3,2},{4,3},{5,4},{6,5},{7,6},{0,7},{9,8},{10,9},{11,1... | collective-permute-start | bytes 1597448 | tf_op jit(solution)/shard_map/ppermute | solution.py:50
  36.3 15.1 %copy-start.3 = (f32[26,8,8,512]{3,2,1,0:T(8,128)S(1)}, f32[26,8,8,512]{3,2,1,0:T(8,128)}, u32[]{:S(2)}) copy-start(f32[26,8,8,512]{3,2,1,0:T(8,128)} %copy-done.2) | copy-start | bytes 10223620
  48.8 15.8 %collective-permute-start.2 = (f32[27,10,1,512]{3,2,1,0:T(1,128)S(1)}, f32[27,10,1,512]{3,2,1,0:T(1,128)S(1)}, u32[]{:S(2)}, u32[]{:S(2)}) collective-permute-start(f32[27,10,1,512]{3,2,1,0:T(1,128)S(1)} %get-tuple-element.102), channel_id=1, source_target_pairs={{0,1},{1,2},{2,3},{3,4},{4,5},{5,6},{6,7},{7,0},{8,9},{9,10},{10,1... | collective-permute-start | bytes 1658888 | tf_op jit(solution)/shard_map/ppermute | solution.py:47
  48.8 15.7 %collective-permute-start.3 = (f32[27,10,1,512]{3,2,1,0:T(1,128)S(1)}, f32[27,10,1,512]{3,2,1,0:T(1,128)S(1)}, u32[]{:S(2)}, u32[]{:S(2)}) collective-permute-start(f32[27,10,1,512]{3,2,1,0:T(1,128)S(1)} %get-tuple-element.103), channel_id=1, source_target_pairs={{1,0},{2,1},{3,2},{4,3},{5,4},{6,5},{7,6},{0,7},{9,8},{10,9},{11,1... | collective-permute-start | bytes 1658888 | tf_op jit(solution)/shard_map/ppermute | solution.py:50
  64.5 21.9 %copy-start.10 = (f32[19,8,8,512]{3,2,1,0:T(8,128)S(1)}, f32[19,8,8,512]{3,2,1,0:T(8,128)}, u32[]{:S(2)}) copy-start(f32[19,8,8,512]{3,2,1,0:T(8,128)} %param.20) | copy-start | bytes 7471108
  64.5 21.9 %copy-start.19 = (f32[7,8,8,512]{3,2,1,0:T(8,128)S(1)}, f32[7,8,8,512]{3,2,1,0:T(8,128)}, u32[]{:S(2)}) copy-start(f32[7,8,8,512]{3,2,1,0:T(8,128)} %param.21) | copy-start | bytes 2752516
  94.5 9.7 %copy-start.5 = (f32[19,8,8,512]{3,2,1,0:T(8,128)}, f32[19,8,8,512]{3,2,1,0:T(8,128)S(1)}, u32[]{:S(2)}) copy-start(f32[19,8,8,512]{3,2,1,0:T(8,128)S(1)} %get-tuple-element.87) | copy-start | bytes 7471108
  101.8 1.7 %copy-start.24 = (f32[19,8,8,512]{3,2,1,0:T(8,128)}, f32[19,8,8,512]{3,2,1,0:T(8,128)S(1)}, u32[]{:S(2)}) copy-start(f32[19,8,8,512]{3,2,1,0:T(8,128)S(1)} %get-tuple-element.83) | copy-start | bytes 7471108
  101.8 1.7 %copy-start.25 = (f32[7,8,8,512]{3,2,1,0:T(8,128)}, f32[7,8,8,512]{3,2,1,0:T(8,128)S(1)}, u32[]{:S(2)}) copy-start(f32[7,8,8,512]{3,2,1,0:T(8,128)S(1)} %get-tuple-element.82) | copy-start | bytes 2752516
  103.6 6.5 %copy-start.11 = (f32[8,8,512]{2,1,0:T(8,128)}, f32[8,8,512]{2,1,0:T(8,128)S(1)}, u32[]{:S(2)}) copy-start(f32[8,8,512]{2,1,0:T(8,128)S(1)} %get-tuple-element.40) | copy-start | bytes 393220
  103.6 8.3 %copy-start.13 = (f32[8,8,512]{2,1,0:T(8,128)}, f32[8,8,512]{2,1,0:T(8,128)S(1)}, u32[]{:S(2)}) copy-start(f32[8,8,512]{2,1,0:T(8,128)S(1)} %get-tuple-element.41) | copy-start | bytes 393220
  104.2 5.9 %copy-start.20 = (f32[8,8,512]{2,1,0:T(8,128)}, f32[8,8,512]{2,1,0:T(8,128)S(1)}, u32[]{:S(2)}) copy-start(f32[8,8,512]{2,1,0:T(8,128)S(1)} %get-tuple-element.47) | copy-start | bytes 393220
  104.2 5.9 %copy-start.33 = (f32[8,8,512]{2,1,0:T(8,128)}, f32[8,8,512]{2,1,0:T(8,128)S(1)}, u32[]{:S(2)}) copy-start(f32[8,8,512]{2,1,0:T(8,128)S(1)} %get-tuple-element.45) | copy-start | bytes 393220
  104.3 7.6 %copy-start.30 = (f32[8,8,512]{2,1,0:T(8,128)}, f32[8,8,512]{2,1,0:T(8,128)S(1)}, u32[]{:S(2)}) copy-start(f32[8,8,512]{2,1,0:T(8,128)S(1)} %get-tuple-element.44) | copy-start | bytes 393220
  107.0 3.2 %copy-start.55 = (f32[7]{0:T(128)S(1)}, f32[7]{0:T(128)}, u32[]{:S(2)}) copy-start(f32[7]{0:T(128)} %constant.100) | copy-start | bytes 88
  107.0 3.2 %copy-start.57 = (f32[7]{0:T(128)S(1)}, f32[7]{0:T(128)}, u32[]{:S(2)}) copy-start(f32[7]{0:T(128)} %constant.99) | copy-start | bytes 88
  107.0 3.2 %copy-start.59 = (f32[7]{0:T(128)S(1)}, f32[7]{0:T(128)}, u32[]{:S(2)}) copy-start(f32[7]{0:T(128)} %constant.98) | copy-start | bytes 88
  107.0 3.2 %copy-start.61 = (f32[7]{0:T(128)S(1)}, f32[7]{0:T(128)}, u32[]{:S(2)}) copy-start(f32[7]{0:T(128)} %constant.56.clone) | copy-start | bytes 88
  107.1 3.2 %copy-start.62 = (f32[7]{0:T(128)S(1)}, f32[7]{0:T(128)}, u32[]{:S(2)}) copy-start(f32[7]{0:T(128)} %constant.104) | copy-start | bytes 88
  107.1 3.1 %copy-start.63 = (f32[7]{0:T(128)S(1)}, f32[7]{0:T(128)}, u32[]{:S(2)}) copy-start(f32[7]{0:T(128)} %constant.103) | copy-start | bytes 88
  107.1 3.1 %copy-start.64 = (f32[7]{0:T(128)S(1)}, f32[7]{0:T(128)}, u32[]{:S(2)}) copy-start(f32[7]{0:T(128)} %constant.102) | copy-start | bytes 88
  110.1 1.8 %copy-start.42 = (f32[8,8,512]{2,1,0:T(8,128)S(1)}, f32[8,8,512]{2,1,0:T(8,128)}, u32[]{:S(2)}) copy-start(f32[8,8,512]{2,1,0:T(8,128)} %param.22) | copy-start | bytes 393220
  110.1 2.5 %copy-start.35 = (pred[32,8,8,512]{3,2,1,0:T(8,128)(4,1)S(1)}, pred[32,8,8,512]{3,2,1,0:T(8,128)(4,1)}, u32[]{:S(2)}) copy-start(pred[32,8,8,512]{3,2,1,0:T(8,128)(4,1)} %copy-done.34) | copy-start | bytes 3145732
  111.9 31.7 %copy-start.12 = (f32[8,8,512]{2,1,0:T(8,128)S(1)}, f32[8,8,512]{2,1,0:T(8,128)}, u32[]{:S(2)}) copy-start(f32[8,8,512]{2,1,0:T(8,128)} %copy-done.11) | copy-start | bytes 393220
  111.9 31.7 %copy-start.17 = (f32[8,8,512]{2,1,0:T(8,128)S(1)}, f32[8,8,512]{2,1,0:T(8,128)}, u32[]{:S(2)}) copy-start(f32[8,8,512]{2,1,0:T(8,128)} %copy-done.15) | copy-start | bytes 393220
  112.6 31.0 %copy-start.14 = (f32[8,8,512]{2,1,0:T(8,128)S(1)}, f32[8,8,512]{2,1,0:T(8,128)}, u32[]{:S(2)}) copy-start(f32[8,8,512]{2,1,0:T(8,128)} %copy-done.13) | copy-start | bytes 393220
  112.6 33.2 %copy-start.23 = (f32[8,8,512]{2,1,0:T(8,128)S(1)}, f32[8,8,512]{2,1,0:T(8,128)}, u32[]{:S(2)}) copy-start(f32[8,8,512]{2,1,0:T(8,128)} %copy-done.22) | copy-start | bytes 393220
  117.7 29.2 %copy-start.21 = (f32[8,8,512]{2,1,0:T(8,128)S(1)}, f32[8,8,512]{2,1,0:T(8,128)}, u32[]{:S(2)}) copy-start(f32[8,8,512]{2,1,0:T(8,128)} %copy-done.20) | copy-start | bytes 393220
  117.7 29.2 %copy-start.27 = (f32[8,8,512]{2,1,0:T(8,128)S(1)}, f32[8,8,512]{2,1,0:T(8,128)}, u32[]{:S(2)}) copy-start(f32[8,8,512]{2,1,0:T(8,128)} %copy-done.26) | copy-start | bytes 393220
  142.3 4.7 %copy-start.29 = (f32[8,8,512]{2,1,0:T(8,128)S(1)}, f32[8,8,512]{2,1,0:T(8,128)}, u32[]{:S(2)}) copy-start(f32[8,8,512]{2,1,0:T(8,128)} %copy-done.28) | copy-start | bytes 393220
  142.3 4.7 %copy-start.31 = (f32[8,8,512]{2,1,0:T(8,128)S(1)}, f32[8,8,512]{2,1,0:T(8,128)}, u32[]{:S(2)}) copy-start(f32[8,8,512]{2,1,0:T(8,128)} %copy-done.30) | copy-start | bytes 393220
  142.3 4.7 %copy-start.32 = (f32[8,8,512]{2,1,0:T(8,128)S(1)}, f32[8,8,512]{2,1,0:T(8,128)}, u32[]{:S(2)}) copy-start(f32[8,8,512]{2,1,0:T(8,128)} %get-tuple-element.34) | copy-start | bytes 393220
  142.3 4.7 %copy-start.37 = (f32[8,8,512]{2,1,0:T(8,128)S(1)}, f32[8,8,512]{2,1,0:T(8,128)}, u32[]{:S(2)}) copy-start(f32[8,8,512]{2,1,0:T(8,128)} %get-tuple-element.11) | copy-start | bytes 393220
  142.3 4.7 %copy-start.38 = (f32[8,8,512]{2,1,0:T(8,128)S(1)}, f32[8,8,512]{2,1,0:T(8,128)}, u32[]{:S(2)}) copy-start(f32[8,8,512]{2,1,0:T(8,128)} %get-tuple-element.32) | copy-start | bytes 393220
  142.3 4.7 %copy-start.39 = (f32[8,8,512]{2,1,0:T(8,128)S(1)}, f32[8,8,512]{2,1,0:T(8,128)}, u32[]{:S(2)}) copy-start(f32[8,8,512]{2,1,0:T(8,128)} %get-tuple-element.26) | copy-start | bytes 393220
  142.3 4.7 %copy-start.40 = (f32[8,8,512]{2,1,0:T(8,128)S(1)}, f32[8,8,512]{2,1,0:T(8,128)}, u32[]{:S(2)}) copy-start(f32[8,8,512]{2,1,0:T(8,128)} %get-tuple-element.28) | copy-start | bytes 393220
  144.6 2.6 %copy-start.6 = (f32[19,8,8,512]{3,2,1,0:T(8,128)S(1)}, f32[19,8,8,512]{3,2,1,0:T(8,128)}, u32[]{:S(2)}) copy-start(f32[19,8,8,512]{3,2,1,0:T(8,128)} %copy-done.5) | copy-start | bytes 7471108
  144.7 2.6 %copy-start.53 = (f32[19]{0:T(128)S(1)}, f32[19]{0:T(128)}, u32[]{:S(2)}) copy-start(f32[19]{0:T(128)} %constant.101) | copy-start | bytes 232
  147.3 2.6 %copy-start.1 = (f32[32]{0:T(128)S(1)}, f32[32]{0:T(128)}, u32[]{:S(2)}) copy-start(f32[32]{0:T(128)} %param.23) | copy-start | bytes 388
  (10 other events, 8.0 us)
